TPU v7x, 32 devices: a whole 2x2x4 slice. The times are simulated.
32 devices in a mesh: grp: 2 (over x), slc: 16 (over z, y, core).
Axes of the slice: x: 2, y: 2, z: 4, core: 2. Of those that a mesh axis runs over, the one named last changes fastest.
Arguments:
- bitstrings: int32 [1024], P('grp'), parts along dimension 0, may hold values from 0 to 511, as said below
- tree_order: int32 [12], P('grp'), parts along dimension 0, may hold values from 0 to 5, each once
- owners: int32 [12], P('grp'), parts along dimension 0, may hold values from 0 to 15
- slice_assign: int32 [64, 6], P(('grp', 'slc')), parts along dimension 0, may hold values from 0 to 63
- boundary: bfloat16 [1024, 4096], P('grp'), parts along dimension 0, may hold values from -6 to 6
- branch_pool: bfloat16 [32, 64, 4096], P(('grp', 'slc')), parts along dimension 0, may hold values from -0.75 to 0.75
- slice_tensors: bfloat16 [12, 64, 4096], P('grp'), parts along dimension 0, may hold values from -3 to 3
- closing: bfloat16 [8192, 128], P('grp'), parts along dimension 0, may hold values from -0.09375 to 0.09375
Outputs:
- amplitudes: float32 [1024, 128], P(('grp', 'slc')), parts along dimension 0
There are 2 independent parts, one for each index of `grp`. A program takes and returns all parts, laid end to end along the dimension named above; each array names one. Nothing has to cross between parts.
Inputs may be any that keep to these rules, and one draw needn't show every extreme that they name: `bitstrings`: 512 distinct configurations. `tree_order`: a permutation of the sections.
All inputs are finite; a program needn't handle non-finite values.
Results may differ from a plain program's by a relative error of at most 0.0075.
Values may be sent and summed in bfloat16 or wider, within the bound.
A program may use at most 128 MiB of HBM per device.

v0:
```python
import math
import jax
import jax.numpy as jnp
from jax import lax
from jax.sharding import PartitionSpec as P


def spread(block, axis, owner):
    block = jnp.where(lax.axis_index(axis) == owner, block, jnp.zeros_like(block))
    return lax.psum(block, axis)


def local(
    bitstrings, tree_order, owners, slice_assign, boundary, branch_pool, slice_tensors, closing
):
    group_count = lax.axis_size("slc")
    my_index = lax.axis_index("slc")
    slice_count = slice_assign.shape[0]
    bond_dim = branch_pool.shape[1]
    pair_dim = branch_pool.shape[2]
    row_total = bitstrings.shape[0]
    section_count = tree_order.shape[0]
    starts = jnp.take(boundary, bitstrings, axis=0)
    states = jnp.broadcast_to(starts[None], (slice_count, row_total, pair_dim))
    own_branch = branch_pool[0]
    for section_idx in range(section_count):
        branch = spread(own_branch, "slc", owners[section_idx])
        product = jnp.einsum(
            "srab,acb->srcb",
            states.reshape(slice_count, row_total, bond_dim, bond_dim),
            branch.reshape(bond_dim, bond_dim, bond_dim),
            preferred_element_type=jnp.float32,
        )
        table = lax.dynamic_index_in_dim(slice_tensors, tree_order[section_idx], 0, keepdims=False)
        factor = jnp.take(table, slice_assign[:, section_idx], axis=0).astype(jnp.float32)
        states = (product.reshape(slice_count, row_total, pair_dim) * factor[:, None, :]).astype(
            jnp.bfloat16
        )
    inverse = 1.0 / math.sqrt(slice_count * group_count)
    share_rows = row_total // group_count
    partial_amps = jnp.einsum("srw,wo->ro", states, closing, preferred_element_type=jnp.float32)
    totals = lax.psum(partial_amps, "slc")
    summed = lax.dynamic_slice_in_dim(totals, my_index * share_rows, share_rows, 0)
    return summed * inverse


def solution(mesh):
    return jax.shard_map(
        local,
        mesh=mesh,
        in_specs=(
            P("grp"),
            P("grp"),
            P("grp"),
            P(("grp", "slc"), None),
            P("grp", None),
            P(("grp", "slc"), None, None),
            P("grp", None, None),
            P("grp", None),
        ),
        out_specs=P(("grp", "slc"), None),
        check_vma=False,
    )
```

profile of v0, /device:TPU:0, one launch (start us, length us, event | category | flops | bytes accessed | tf_op | source)
XLA Modules:
  0.0 318.7 jit_solution(11319033203107848922)
XLA Ops:
  6.5 1.5 fusion.25
  11.9 2.4 broadcast_select_fusion.6
  14.3 2.1 reshape.99
  16.3 2.9 copy.34
  19.3 2.1 reshape.102
  21.3 2.9 copy.37
  24.2 2.1 reshape.101
  26.3 2.9 copy.36
  29.2 2.1 reshape.100
  31.3 2.9 copy.35
  34.2 1.1 reshape.104
  35.3 2.9 copy.39
  38.2 1.1 reshape.103
  39.4 2.9 copy.38
  42.3 0.2 all-reduce.4.cloned.1.call-start
  42.6 0.7 fusion.24
  50.8 0.3 slice_reduce_fusion.1
  55.0 3.2 dynamic-slice_bitcast_fusion.1
  58.2 1.7 gather_fusion.5
  60.0 0.1 reshape.115
  60.1 0.1 copy.46
  60.2 1.7 gather_fusion.4
  62.0 0.1 reshape.114
  62.1 0.1 copy.45
  62.2 0.6 gather_fusion.3
  62.9 0.1 reshape.113
  63.0 0.1 copy.44
  63.1 0.6 gather_fusion.2
  63.7 0.1 reshape.112
  63.8 0.1 copy.43
  63.9 0.6 gather_fusion.1
  64.6 0.1 reshape.111
  64.7 0.1 copy.42
  64.8 0.6 gather_fusion.6
  65.5 0.1 reshape.116
  65.6 0.1 copy.47
  65.7 11.4 %gather_fusion = bf16[512,4096]{1,0:T(8,128)(2,1)} fusion(bf16[512,4096]{1,0:T(8,128)(2,1)} %param.14, s32[1024]{0:T(1024)S(1)} %pad_clamp_fusion.6), kind=kCustom, calls=%fused_computation.6 | custom fusion | bytes 8390656 | tf_op jit(solution)/shard_map/jit(_take)/gather | solution.py:23
  77.1 6.5 %copy.40 = bf16[512,4096]{0,1:T(8,128)(2,1)} copy(bf16[512,4096]{1,0:T(8,128)(2,1)} %gather_fusion) | data formatting | bytes 8388608 | tf_op jit(solution)/shard_map/jit(_take)/gather | solution.py:23
  83.6 2.7 broadcast_select_fusion
  86.3 4.4 %copy.41 = bf16[512,64,64]{0,1,2:T(8,128)(2,1)} copy(bf16[512,64,64]{0,2,1:T(8,128)(2,1)S(1)} %broadcast_select_fusion) | data formatting | bytes 8388608 | tf_op jit(solution)/shard_map/jit(_take)/select_n | solution.py:23
  90.7 94.3 %all-reduce.6.cloned.1.call-done = (bf16[64,64,64]{0,1,2:T(8,128)(2,1)}, bf16[64,64,64]{0,1,2:T(8,128)(2,1)}, bf16[64,64,64]{0,1,2:T(8,128)(2,1)}, bf16[64,64,64...) async-done(((bf16[64,64,64]{0,1,2:T(8,128)(2,1)}, bf16[64,64,64]{0,1,2:T(8,128)(2,1)}, bf16[64,64,64]{0,1,2:T(8,128)(2,1)}, ...) | async-done | bytes 3145744 | tf_op jit(solution)/shard_map/psum | solution.py:10
  185.0 8.7 %fusion.4 = bf16[2,512,64,64]{1,2,0,3:T(8,128)(2,1)} fusion(f32[2,64,64]{1,0,2:T(2,128)S(1)} %copy.43, f32[2,64,64]{1,0,2:T(2,128)S(1)} %copy.42, bf16[512,64,64]{0,1,2:T(8,128)(2,1)} %copy.41, bf16[64,64,64]{0,1,2:T(8,128)(2,1)} %get-tuple-element.12, bf16[64,64,64]{0,1,2:T(8,128)(2,1)} %get-tuple-element.13), kind=kOutput, calls=%fused_computation.16 | convolution fusion | flops 1090519040 | bytes 13697024 | tf_op jit(solution)/shard_map/srab,acb->srcb/dot_general | solution.py:28
  193.7 9.8 %fusion.2 = bf16[2,512,64,64]{1,2,0,3:T(8,128)(2,1)} fusion(f32[2,64,64]{1,0,2:T(2,128)S(1)} %copy.45, bf16[2,512,64,64]{1,2,0,3:T(8,128)(2,1)} %fusion.4, f32[2,64,64]{1,0,2:T(2,128)S(1)} %copy.44, bf16[64,64,64]{0,1,2:T(8,128)(2,1)S(1)} %copy-done.1, bf16[64,64,64]{0,1,2:T(8,128)(2,1)S(1)} %copy-done.2), kind=kOutput, calls=%fused_computation.12 | convolution fusion | flops 1090519040 | bytes 17891328 | tf_op jit(solution)/shard_map/srab,acb->srcb/dot_general | solution.py:28
  203.5 10.4 %convert_reduce_fusion = bf16[512,64,64]{0,1,2:T(8,128)(2,1)} fusion(f32[2,64,64]{1,0,2:T(2,128)S(1)} %copy.47, bf16[2,512,64,64]{1,2,0,3:T(8,128)(2,1)} %fusion.2, f32[2,64,64]{1,0,2:T(2,128)S(1)} %copy.46, bf16[64,64,64]{0,1,2:T(8,128)(2,1)} %get-tuple-element.16, bf16[64,64,64]{0,1,2:T(8,128)(2,1)} %get-tuple-element.17), kind=kOutput, calls=%fused_computation.19 | convolution fusion | flops 1096810496 | bytes 13697024 | tf_op jit(solution)/shard_map/srab,acb->srcb/dot_general | solution.py:28
  213.9 4.5 %copy.48 = bf16[512,64,64]{0,2,1:T(8,128)(2,1)S(1)} copy(bf16[512,64,64]{0,1,2:T(8,128)(2,1)} %convert_reduce_fusion) | data formatting | bytes 8388608 | tf_op jit(solution)/shard_map/srw,wo->ro/reduce_sum | solution.py:41
  218.4 2.0 fusion.26
  220.5 90.1 %all-reduce.4.cloned.1.call-done = f32[512,128]{1,0:T(8,128)} async-done(((f32[512,128]{1,0:T(8,128)}), f32[512,128]{1,0:T(8,128)}) %all-reduce.4.cloned.1.call-update) | async-done | bytes 262160 | tf_op jit(solution)/shard_map/psum | solution.py:42
  310.5 1.3 dynamic-slice_multiply_fusion
  (36 shorter events, 0.7 us)
Async XLA Ops:
  6.5 211.9 %copy-start = (bf16[4096,128]{1,0:T(8,128)(2,1)S(1)}, bf16[4096,128]{1,0:T(8,128)(2,1)}, u32[]{:S(2)}) copy-start(bf16[4096,128]{1,0:T(8,128)(2,1)} %param.17) | copy-start | bytes 3145732
  6.5 178.4 %all-reduce.6.cloned.1.call-start = ((), (), s32[]{:S(2)}) async-start(), calls=%async_computation.1 | async-start | bytes 12582912 | tf_op jit(solution)/shard_map/psum | solution.py:10
  29.2 13.4 %copy-start.4 = (s32[6]{0:T(128)S(1)}, s32[6]{0:T(128)}, u32[]{:S(2)}) copy-start(s32[6]{0:T(128)} %param.11) | copy-start | bytes 76
  29.2 21.6 %copy-start.3 = (s32[2,6]{1,0:T(2,128)S(1)}, s32[2,6]{1,0:T(2,128)}, u32[]{:S(2)}) copy-start(s32[2,6]{1,0:T(2,128)} %param.13) | copy-start | bytes 148
  39.4 26.3 %copy-start.5 = (s32[512]{0:T(512)S(1)}, s32[512]{0:T(512)}, u32[]{:S(2)}) copy-start(s32[512]{0:T(512)} %param.10) | copy-start | bytes 6148
  42.3 268.2 %all-reduce.4.cloned.1.call-start = ((), (), s32[]{:S(2)}) async-start(), calls=%async_computation | async-start | bytes 524288 | tf_op jit(solution)/shard_map/psum | solution.py:42
  185.0 8.7 %copy-start.1 = (bf16[64,64,64]{0,1,2:T(8,128)(2,1)S(1)}, bf16[64,64,64]{0,1,2:T(8,128)(2,1)}, u32[]{:S(2)}) copy-start(bf16[64,64,64]{0,1,2:T(8,128)(2,1)} %get-tuple-element.14) | copy-start | bytes 1572868
  185.0 8.7 %copy-start.2 = (bf16[64,64,64]{0,1,2:T(8,128)(2,1)S(1)}, bf16[64,64,64]{0,1,2:T(8,128)(2,1)}, u32[]{:S(2)}) copy-start(bf16[64,64,64]{0,1,2:T(8,128)(2,1)} %get-tuple-element.15) | copy-start | bytes 1572868
Sparse Core Ops, SparseCore 0:
  42.4 142.4 all-reduce.5
  220.6 89.9 all-reduce.3
where the time goes:
time: 320 us; the launch traced here: 319 us
  waiting for transfers between devices  184 us (58%)
  local copies, waits for them, and re-layouts  67.4 us (21%)
  matrix products  30.9 us (10%)
  between operations  28.8 us (9%)
  other arithmetic  7.02 us (2%)
    psum x1, waiting for transfers between devices, spread(): return lax.psum(block, axis)  94.3 us
    psum x1, waiting for transfers between devices, local(): totals = lax.psum(partial_amps, 'slc')  90.1 us
    dot_general x3, matrix products, local(): jnp.einsum('srab,acb->srcb', states.reshape(slice_count, row_total, bond_...  28.9 us
    reshape x12, local copies, waits for them, and re-layouts, local(): branch.reshape(bond_dim, bond_dim, bond_dim)  28 us
    gather x2, local copies, waits for them, and re-layouts, local(): starts = jnp.take(boundary, bitstrings, axis=0)  17.9 us
  transfers between devices with their start and end apart: 2, of which 2 were waited for; matrix products, arithmetic and copies ran while one was open for 11% of the time, Pallas kernels for 0%

commit v1 on v0

--- a/solution.py
+++ b/solution.py
@@ -7,7 +7,7 @@
 
 def spread(block, axis, owner):
     block = jnp.where(lax.axis_index(axis) == owner, block, jnp.zeros_like(block))
-    return lax.psum(block, axis)
+    return jnp.sum(lax.all_gather(block, axis), axis=0)
 
 
 def local(

time: 320 us -> 615 us (1.92)
  waiting for transfers between devices: 184 us -> 440 us
  other arithmetic: 7.02 us -> 38.9 us
    all_gather x0 -> x6, waiting for transfers between devices: none -> 348 us  [spread(): return jnp.sum(lax.all_gather(block, axis), axis=0)]
    psum x1 -> x0, waiting for transfers between devices: 94.3 us -> none  [spread(): return lax.psum(block, axis)]
    reduce_sum x0 -> x6, other arithmetic: none -> 31.6 us  [spread(): return jnp.sum(lax.all_gather(block, axis), axis=0)]
  transfers between devices with their start and end apart: 2 -> 7, of which waited for: 2 -> 7; matrix products, arithmetic and copies ran while one was open for 11% -> 15% of each run, Pallas kernels for 0% -> 0%
where the time goes in v1:
time: 615 us; the launch traced here: 612 us
  waiting for transfers between devices  440 us (72%)
  local copies, waits for them, and re-layouts  72.6 us (12%)
  other arithmetic  38.9 us (6%)
  matrix products  30.7 us (5%)
  between operations  29.4 us (5%)
    all_gather x6, waiting for transfers between devices, spread(): return jnp.sum(lax.all_gather(block, axis), axis=0)  348 us
    psum x1, waiting for transfers between devices, local(): totals = lax.psum(partial_amps, 'slc')  88.5 us
    reduce_sum x6, other arithmetic, spread(): return jnp.sum(lax.all_gather(block, axis), axis=0)  31.6 us
    reshape x12, local copies, waits for them, and re-layouts, local(): branch.reshape(bond_dim, bond_dim, bond_dim)  31.1 us
    dot_general x3, matrix products, local(): jnp.einsum('srab,acb->srcb', states.reshape(slice_count, row_total, bond_...  28.8 us
    gather x2, local copies, waits for them, and re-layouts, local(): starts = jnp.take(boundary, bitstrings, axis=0)  18.3 us
  transfers between devices with their start and end apart: 7, of which 7 were waited for; matrix products, arithmetic and copies ran while one was open for 15% of the time, Pallas kernels for 0%

profile of v1, /device:TPU:0, one launch (start us, length us, event | category | flops | bytes accessed | tf_op | source)
XLA Modules:
  0.0 611.6 jit_solution(12091295502555042793)
XLA Ops:
  6.5 1.5 fusion.16
  11.9 2.8 broadcast_select_fusion.1
  14.7 0.7 all-gather.15.cloned.1.call-update
  15.4 0.7 all-gather.13.cloned.1.call-update
  17.9 1.6 fusion.15
  31.1 1.2 slice_reduce_fusion.1
  32.3 3.1 dynamic-slice_bitcast_fusion.1
  35.3 1.7 gather_fusion.1
  37.4 1.7 gather_fusion.2
  39.4 11.7 %gather_fusion = bf16[512,4096]{1,0:T(8,128)(2,1)} fusion(bf16[512,4096]{1,0:T(8,128)(2,1)} %param.14, s32[1024]{0:T(1024)S(1)} %pad_clamp_fusion.6), kind=kCustom, calls=%fused_computation.6 | custom fusion | bytes 8390656 | tf_op jit(solution)/shard_map/jit(_take)/gather | solution.py:23
  51.1 6.7 %copy.34 = bf16[512,4096]{0,1:T(8,128)(2,1)} copy(bf16[512,4096]{1,0:T(8,128)(2,1)} %gather_fusion) | data formatting | bytes 8388608 | tf_op jit(solution)/shard_map/jit(_take)/gather | solution.py:23
  57.7 2.6 broadcast_select_fusion
  60.4 4.4 copy.35
  64.8 0.6 gather_fusion.3
  65.7 0.6 gather_fusion.4
  66.6 0.6 gather_fusion.5
  67.5 0.6 gather_fusion.6
  68.4 23.4 %all-gather.17.cloned.1.call-done = bf16[16,64,4096]{2,1,0:T(8,128)(2,1)} async-done(((bf16[1,64,4096]{2,1,0:T(8,128)(2,1)}), bf16[16,64,4096]{2,1,0:T(8,128)(2,1)}) %all-gather.17.cloned.1.call-update) | async-done | bytes 8388624 | tf_op jit(solution)/shard_map/all_gather | solution.py:10
  91.8 5.0 reduce_sum.88
  96.8 1.1 reshape.86
  97.9 3.4 copy.49
  101.4 65.5 %all-gather.15.cloned.1.call-done = bf16[16,64,4096]{2,1,0:T(8,128)(2,1)} async-done(((bf16[1,64,4096]{2,1,0:T(8,128)(2,1)}), bf16[16,64,4096]{2,1,0:T(8,128)(2,1)}) %all-gather.15.cloned.1.call-update) | async-done | bytes 8388624 | tf_op jit(solution)/shard_map/all_gather | solution.py:10
  166.9 5.0 reduce_sum.87
  171.9 1.1 reshape.85
  173.0 2.9 copy.50
  176.0 66.0 %all-gather.13.cloned.1.call-done = bf16[16,64,4096]{2,1,0:T(8,128)(2,1)} async-done(((bf16[1,64,4096]{2,1,0:T(8,128)(2,1)}), bf16[16,64,4096]{2,1,0:T(8,128)(2,1)}) %all-gather.13.cloned.1.call-update) | async-done | bytes 8388624 | tf_op jit(solution)/shard_map/all_gather | solution.py:10
  242.0 5.0 reduce_sum.86
  247.0 1.1 reshape.84
  248.1 2.2 copy.51
  250.3 66.6 %all-gather.11.cloned.1.call-done = bf16[16,64,4096]{2,1,0:T(8,128)(2,1)} async-done(((bf16[1,64,4096]{2,1,0:T(8,128)(2,1)}), bf16[16,64,4096]{2,1,0:T(8,128)(2,1)}) %all-gather.11.cloned.1.call-update) | async-done | bytes 8388624 | tf_op jit(solution)/shard_map/all_gather | solution.py:10
  316.9 5.0 reduce_sum.85
  321.9 2.1 reshape.83
  324.0 3.5 copy.52
  327.5 64.3 %all-gather.9.cloned.1.call-done = bf16[16,64,4096]{2,1,0:T(8,128)(2,1)} async-done(((bf16[1,64,4096]{2,1,0:T(8,128)(2,1)}), bf16[16,64,4096]{2,1,0:T(8,128)(2,1)}) %all-gather.9.cloned.1.call-update) | async-done | bytes 8388624 | tf_op jit(solution)/shard_map/all_gather | solution.py:10
  391.8 5.9 reduce_sum.84
  397.7 2.7 reshape.82
  400.4 4.0 copy.53
  404.4 62.3 %all-gather.7.cloned.1.call-done = bf16[16,64,4096]{2,1,0:T(8,128)(2,1)} async-done(((bf16[1,64,4096]{2,1,0:T(8,128)(2,1)}), bf16[16,64,4096]{2,1,0:T(8,128)(2,1)}) %all-gather.7.cloned.1.call-update) | async-done | bytes 8388624 | tf_op jit(solution)/shard_map/all_gather | solution.py:10
  466.8 5.9 reduce_sum.83
  472.6 2.8 reshape.81
  475.4 4.0 copy.54
  479.4 8.6 %fusion.4 = bf16[2,512,64,64]{1,2,0,3:T(8,128)(2,1)} fusion(bf16[64,64,64,1]{0,1,3,2:T(8,128)(2,1)} %copy.50, f32[2,64,64]{1,0,2:T(2,128)S(1)} %copy.39, bf16[64,64,64,1]{0,1,3,2:T(8,128)(2,1)} %copy.49, f32[2,64,64]{1,0,2:T(2,128)S(1)} %copy.37, bf16[512,64,64]{0,1,2:T(8,128)(2,1)} %copy.35), kind=kOutput, calls=%fused_computation.16 | convolution fusion | flops 1090519040 | bytes 13697024 | tf_op jit(solution)/shard_map/srab,acb->srcb/dot_general | solution.py:28
  488.0 10.0 %fusion.2 = bf16[2,512,64,64]{1,2,0,3:T(8,128)(2,1)} fusion(bf16[64,64,64,1]{0,1,3,2:T(8,128)(2,1)S(1)} %copy.52, f32[2,64,64]{1,0,2:T(2,128)S(1)} %copy.43, bf16[64,64,64,1]{0,1,3,2:T(8,128)(2,1)S(1)} %copy.51, bf16[2,512,64,64]{1,2,0,3:T(8,128)(2,1)} %fusion.4, f32[2,64,64]{1,0,2:T(2,128)S(1)} %copy.41), kind=kOutput, calls=%fused_computation.12 | convolution fusion | flops 1090519040 | bytes 17891328 | tf_op jit(solution)/shard_map/srab,acb->srcb/dot_general | solution.py:28
  498.0 10.2 %convert_reduce_fusion = bf16[512,64,64]{0,1,2:T(8,128)(2,1)} fusion(f32[2,64,64]{1,0,2:T(2,128)S(1)} %copy.47, bf16[64,64,64,1]{0,1,3,2:T(8,128)(2,1)} %copy.54, bf16[64,64,64,1]{0,1,3,2:T(8,128)(2,1)} %copy.53, bf16[2,512,64,64]{1,2,0,3:T(8,128)(2,1)} %fusion.2, f32[2,64,64]{1,0,2:T(2,128)S(1)} %copy.45), kind=kOutput, calls=%fused_computation.19 | convolution fusion | flops 1096810496 | bytes 13697024 | tf_op jit(solution)/shard_map/srab,acb->srcb/dot_general | solution.py:28
  508.1 4.5 copy.48
  512.7 2.0 fusion.17
  514.7 88.5 %all-reduce.2.cloned.1.call-done = f32[512,128]{1,0:T(8,128)} async-done(((f32[512,128]{1,0:T(8,128)}), f32[512,128]{1,0:T(8,128)}) %all-reduce.2.cloned.1.call-update) | async-done | bytes 262160 | tf_op jit(solution)/shard_map/psum | solution.py:42
  603.2 1.3 dynamic-slice_multiply_fusion
  (49 shorter events, 3.6 us)
Async XLA Ops:
  6.5 506.1 %copy-start = (bf16[4096,128]{1,0:T(8,128)(2,1)S(1)}, bf16[4096,128]{1,0:T(8,128)(2,1)}, u32[]{:S(2)}) copy-start(bf16[4096,128]{1,0:T(8,128)(2,1)} %param.17) | copy-start | bytes 3145732
  6.5 32.8 %copy-start.1 = (s32[512]{0:T(512)S(1)}, s32[512]{0:T(512)}, u32[]{:S(2)}) copy-start(s32[512]{0:T(512)} %param.10) | copy-start | bytes 6148
  6.5 85.3 %all-gather.17.cloned.1.call-start = ((), (), s32[]{:S(2)}) async-start(), calls=%async_computation.5 | async-start | bytes 8912896 | tf_op jit(solution)/shard_map/all_gather | solution.py:10
  14.6 152.3 %all-gather.15.cloned.1.call-start = ((), (), s32[]{:S(2)}) async-start(), calls=%async_computation.4 | async-start | bytes 8912896 | tf_op jit(solution)/shard_map/all_gather | solution.py:10
  15.4 226.6 %all-gather.13.cloned.1.call-start = ((), (), s32[]{:S(2)}) async-start(), calls=%async_computation.3 | async-start | bytes 8912896 | tf_op jit(solution)/shard_map/all_gather | solution.py:10
  16.1 300.8 %all-gather.11.cloned.1.call-start = ((), (), s32[]{:S(2)}) async-start(), calls=%async_computation.2 | async-start | bytes 8912896 | tf_op jit(solution)/shard_map/all_gather | solution.py:10
  16.7 375.1 %all-gather.9.cloned.1.call-start = ((), (), s32[]{:S(2)}) async-start(), calls=%async_computation.1 | async-start | bytes 8912896 | tf_op jit(solution)/shard_map/all_gather | solution.py:10
  17.3 449.5 %all-gather.7.cloned.1.call-start = ((), (), s32[]{:S(2)}) async-start(), calls=%async_computation | async-start | bytes 8912896 | tf_op jit(solution)/shard_map/all_gather | solution.py:10
  17.9 585.3 %all-reduce.2.cloned.1.call-start = ((), (), s32[]{:S(2)}) async-start(), calls=%async_computation.6 | async-start | bytes 524288 | tf_op jit(solution)/shard_map/psum | solution.py:42
Sparse Core Ops, SparseCore 0:
  14.8 77.0 all-gather.16
  94.0 72.8 all-gather.14
  169.1 72.8 all-gather.12
  244.0 72.8 all-gather.10
  318.9 72.8 all-gather.8
  393.9 72.8 all-gather.6
  514.8 88.3 all-reduce.1
